TPU v7x, 32 devices: a whole 2x2x4 slice. The times are simulated.
32 devices in a mesh: fsdp: 16 (over z, y, core), dp: 2 (over x).
Axes of the slice: x: 2, y: 2, z: 4, core: 2. Of those that a mesh axis runs over, the one named last changes fastest.
Arguments:
- tokens: bfloat16 [32768, 1024], P(('fsdp', 'dp')), may hold values from -6 to 6
- item_start: int32 [32768], P(('fsdp', 'dp')), may hold values from 0 to 896, as said below
- out_grad: bfloat16 [32768, 1024], P(('fsdp', 'dp')), may hold values from -6 to 6
- norm_gains: float32 [2, 1024], replicated, may hold values from 0.5 to 1.5
- norm_shifts: float32 [2, 1024], replicated, may hold values from -1.25 to 1.25
- w_qkv: bfloat16 [1024, 3072], P('fsdp'), may hold values from -0.1875 to 0.1875
- bias_qkv: float32 [3072], replicated, may hold values from -1.25 to 1.25
- w_out: bfloat16 [1024, 1024], P('fsdp'), may hold values from -0.5 to 0.5
- w_fc: bfloat16 [1024, 4096], P('fsdp'), may hold values from -0.1875 to 0.1875
- bias_fc: float32 [4096], replicated, may hold values from -1.75 to 1.75
- w_proj: bfloat16 [4096, 1024], P('fsdp'), may hold values from -0.09375 to 0.09375
- out_biases: float32 [2, 1024], replicated, may hold values from -1.25 to 1.25
- adapters: float32 [4, 1024, 4], replicated, may hold values from -0.3125 to 0.3125
- momentum: float32 [4, 1024, 4], replicated, may hold values from -1280 to 1280
- average: float32 [4, 1024, 4], replicated, may hold values from -0.3125 to 0.3125
Outputs:
- block_out: bfloat16 [32768, 1024], P(('fsdp', 'dp'))
- in_grad: float32 [32768, 1024], P(('fsdp', 'dp'))
- adapter_grad: float32 [4, 1024, 4], replicated
- new_momentum: float32 [4, 1024, 4], replicated
- new_adapters: float32 [4, 1024, 4], replicated
- new_average: float32 [4, 1024, 4], replicated
- adapter_copy: bfloat16 [4, 1024, 4], replicated
Inputs may be any that keep to these rules, and one draw needn't show every extreme that they name: `item_start`: each device's 1024 rows are cut into aligned runs of 1024 rows, and each run into items of 1024, 512, 256 or 128 rows at aligned places; every row holds the first row of its item, counted within its device. Every draw has an item of 1024 rows and one of 128 rows.
All inputs are finite; a program needn't handle non-finite values.
Results may differ from a plain program's by a relative error of at most 0.014.
The roundings to bfloat16 on the way count: a program that leaves them out, or rounds other values in their place, can miss the bound.
Values may be sent and summed in bfloat16 or wider, within the bound.
A program may use at most 256 MiB of HBM per device.

v0:
```python
import functools
import math
import jax, jax.numpy as jnp
from jax import lax
from jax.experimental import pallas as pl
from jax.experimental.pallas import tpu as pltpu
from jax.sharding import PartitionSpec as P
F32=jnp.float32; BF=jnp.bfloat16
T=1024; D=1024; H=16; G=4; GW=256
NEG=-1e30
def nn(a,b): return lax.dot_general(a,b,(((1,),(0,)),((),())),preferred_element_type=F32)
def nt(a,b): return lax.dot_general(a,b,(((1,),(1,)),((),())),preferred_element_type=F32)
def tn(a,b): return lax.dot_general(a,b,(((0,),(0,)),((),())),preferred_element_type=F32)
def lane(shape): return lax.broadcasted_iota(jnp.int32,shape,1)
def row(shape): return lax.broadcasted_iota(jnp.int32,shape,0)
def stats(v):
    mu=jnp.mean(v,axis=-1,keepdims=True); c=v-mu
    rs=lax.rsqrt(jnp.mean(c*c,axis=-1,keepdims=True)+1e-5)
    return c,rs
def parts(x):
    hi=x.astype(BF); r1=x-hi.astype(F32); mid=r1.astype(BF); lo=(r1-mid.astype(F32)).astype(BF)
    return hi.astype(F32),mid.astype(F32),lo.astype(F32)
def key_lanes(starts_row):
    l=lane((T,128)); r=row((T,128))
    return jnp.where(l<8, jnp.where(r>=starts_row,0.0,NEG), jnp.where(l<11,-1.0,0.0)).astype(BF)
def query_lanes(cols):
    l=lane((T,128)); r=row((T,128))
    base=jnp.where(l==lax.shift_right_logical(r,7),1.0,0.0)
    if cols is not None:
        hi,mid,lo=cols
        base=jnp.where(l==8,hi,jnp.where(l==9,mid,jnp.where(l==10,lo,base)))
    return base.astype(BF)
QB=256
VM=pl.BlockSpec(memory_space=pltpu.VMEM)
C0=0.7978845608; C1=0.044715
def attn_bwd_pair(q,k,v,do,o,lcols,klanes,store,KB=256):
    l=lane((T,128))
    q8=q*jnp.asarray(0.125,BF)
    ka=jnp.concatenate([k,klanes],axis=1)
    vl=jnp.where((l>=8)&(l<11),-1.0,0.0).astype(BF)
    va=jnp.concatenate([v,vl],axis=1)
    prod=do.astype(F32)*o.astype(F32)
    causal=row((KB,KB))<=lane((KB,KB))
    res=[]
    for h in range(2):
        hm=(l<64) if h==0 else (l>=64)
        dcol=jnp.sum(jnp.where(hm,prod,0.0),axis=1,keepdims=True)
        qa=jnp.concatenate([jnp.where(hm,q8,jnp.zeros_like(q8)),query_lanes(parts(lcols[h]))],axis=1)
        hi,mid,lo=parts(dcol)
        dl=jnp.where(l==8,hi,jnp.where(l==9,mid,jnp.where(l==10,lo,0.0))).astype(BF)
        da=jnp.concatenate([jnp.where(hm,do,jnp.zeros_like(do)),dl],axis=1)
        dqs=[None]*(T//KB); dks=[];dvs=[]
        for j in range(T//KB):
            r0=j*KB
            t=nt(ka[r0:r0+KB],qa[r0:])
            td=jnp.where(causal,t[:,:KB],NEG)
            t=jnp.concatenate([td,t[:,KB:]],axis=1) if r0+KB<T else td
            p=jnp.exp(t)
            dvs.append(nn(p.astype(BF),do[r0:]))
            u=nt(va[r0:r0+KB],da[r0:])
            ds=(p*u).astype(BF)
            dks.append(nn(ds,q8[r0:]))
            dq=tn(ds,k[r0:r0+KB])
            for i in range(j,T//KB):
                piece=dq[(i-j)*KB:(i-j+1)*KB]
                dqs[i]=piece if dqs[i] is None else dqs[i]+piece
        res.append((dqs,dks,dvs))
    lk=lane((KB,128))<64
    for i in range(T//KB):
        sl=slice(i*KB,(i+1)*KB)
        store("q",sl,jnp.where(lk,res[0][0][i],res[1][0][i])*0.125)
        store("k",sl,jnp.where(lk,res[0][1][i],res[1][1][i]))
        store("v",sl,jnp.where(lk,res[0][2][i],res[1][2][i]))
MESH=pl.DeviceIdType.MESH

NU=12; NC=24; LEAD=3; OFFS=(-LEAD,0,2,4); XC=384
class Gather:
    def __init__(self,A,B,l_ref,u_ref,S):
        self.l,self.u,self.S=l_ref,u_ref,S
        self.hr=u_ref.shape[4]//2
        f=lax.axis_index("fsdp"); d=lax.axis_index("dp")
        self.c=f&1; h=f>>1; self.b=h&(B-1); self.a=h>>(B.bit_length()-1)
        par=d&1
        def dev(a,b,c,e): return {"fsdp":(a*B+b)*2+c,"dp":e}
        self.long_a=A>=B; self.L1,self.L2=(A,B) if A>=B else (B,A)
        def along_a(k): return (self.a+k)&(A-1),self.b
        def along_b(k): return self.a,(self.b+k)&(B-1)
        l1,l2=(along_a,along_b) if self.long_a else (along_b,along_a)
        self.p1=[l1(k) for k in range(1,self.L1)]; self.p2=[l2(k) for k in range(1,self.L2)]
        self.d1=[dev(*p,self.c,d) for p in self.p1]; self.d2=[dev(*p,self.c,d) for p in self.p2]
        self.dx=dev(self.a,self.b,self.c,d+1-2*par); self.dc=dev(self.a,self.b,1-self.c,d)
        self.carried=pl.ds(pl.multiple_of(par*XC,128),D-XC)
        self.crossed=pl.ds(pl.multiple_of(par*(D-XC),128),XC)
        self.peers=[self.dc,self.dx]+self.d1+self.d2
    def greet(self):
        self.bar=pltpu.get_barrier_semaphore()
        for p in self.peers: pl.semaphore_signal(self.bar,inc=1,device_id=p,device_id_type=MESH)
    def greeted(self): pl.semaphore_wait(self.bar,len(self.peers))
    def rows(self,g): return g>>1,pl.ds(pl.multiple_of((g&1)*self.hr,8),self.hr)
    def own(self,lo,hi,k): return pltpu.make_async_copy(self.l.at[lo:hi],self.u.at[lo:hi,self.a,self.b,self.c],self.S["loc"].at[k])
    def rc(self,src,dst,name,g,to):
        return pltpu.make_async_remote_copy(src_ref=src,dst_ref=dst,send_sem=self.S[name+"s"],recv_sem=self.S[name+"r"].at[g],device_id=to,device_id_type=MESH)
    def col(self,b,r,cols,u):
        return self.u.at[u,:,b,self.c,r,cols] if self.long_a else self.u.at[u,b,:,self.c,r,cols]
    def zs(self,g):
        u,r=self.rows(g); s=self.l.at[u,r,self.carried]; t=self.u.at[u,self.a,self.b,self.c,r,self.carried]
        return [self.rc(s,t,"z",g,e) for e in self.d1]
    def ys(self,g):
        u,r=self.rows(g); v=self.col(self.b if self.long_a else self.a,r,self.carried,u)
        return [self.rc(v,v,"y",g,e) for e in self.d2]
    def xs(self,g):
        u,r=self.rows(g); out=[]
        for p in self.p1:
            v=self.u.at[u,p[0],p[1],self.c,r,self.crossed]; out.append(self.rc(v,v,"x",g,self.dx))
        return out
    def ws(self,g):
        u,r=self.rows(g); out=[]
        for p in self.p2:
            v=self.col(p[1] if self.long_a else p[0],r,self.crossed,u); out.append(self.rc(v,v,"w",g,self.dx))
        return out
    def cs(self,g):
        u,r=self.rows(g); v=self.u.at[u,:,:,self.c,r]
        return [self.rc(v,v,"c",g,self.dc)]
    def box(self,name,u,r):
        n1=slice(0,self.L1-1); n2=slice(0,self.L2-1); al=slice(None)
        m={"z":(n1,0,self.carried),"y":(al,n2,self.carried),"x":(n1,0,self.crossed),"w":(al,n2,self.crossed),"c":(al,al,al)}[name]
        i1,i2=(m[0],m[1]) if self.long_a else (m[1],m[0])
        return self.u.at[u,i1,i2,0,r,m[2]]
    def got(self,name,g):
        u,r=self.rows(g); v=self.box(name,u,r)
        self.rc(v,v,name,g,self.dc).wait_recv()
    def stage(self,s,g):
        if s==0:
            for cp in self.zs(g): cp.start()
        elif s==1:
            self.got("z",g)
            for cp in self.ys(g)+self.xs(g): cp.start()
        elif s==2:
            self.got("y",g)
            for cp in self.ws(g): cp.start()
        else:
            self.got("x",g); self.got("w",g)
            for cp in self.cs(g): cp.start()
    def tick(self,t,safe=False,least=0):
        for s,o in enumerate(OFFS):
            if isinstance(t,int):
                if (2 if s==3 else 0)<=t-o<NC: self.stage(s,jnp.int32(t-o))
            elif safe and s<3: self.stage(s,t-o)
            elif safe:
                @pl.when(t-o>=least)
                def _(s=s,o=o): self.stage(s,t-o)
            else:
                @pl.when(t-o<NC)
                def _(s=s,o=o): self.stage(s,t-o)
    def ready(self,u):
        self.got("c",2*u); self.got("c",2*u+1)
    def finish(self):
        for n in "zyxwc":
            v=self.box(n,slice(None),slice(None))
            self.rc(v,v,n,0,self.dc).wait_send()
    @staticmethod
    def sems(A,B):
        s={"loc":(2,)}
        for n in "zyxwc": s[n+"s"]=(); s[n+"r"]=(NC,)
        return {n:pltpu.SemaphoreType.DMA(v) for n,v in s.items()}

def attn_fwd_head(q8,k,v,klanes,qlanes,h,put):
    l=lane((T,128))
    hm=(l<64) if h==0 else (l>=64)
    qa=jnp.concatenate([jnp.where(hm,q8,jnp.zeros_like(q8)),qlanes],axis=1)
    ka=jnp.concatenate([k,klanes],axis=1)
    tri=lane((QB,QB))<=row((QB,QB))
    for i in range(T//QB):
        n=(i+1)*QB
        s=nt(qa[i*QB:(i+1)*QB],ka[:n])
        sd=jnp.where(tri,s[:,n-QB:],NEG)
        s=jnp.concatenate([s[:,:n-QB],sd],axis=1) if i else sd
        m=jnp.max(s,axis=1,keepdims=True)
        e=jnp.exp(s-m)
        tot=jnp.sum(e,axis=1,keepdims=True)
        put(i,nn(e.astype(BF),v[:n])*(1.0/tot),m+jnp.log(tot))

def spread(piece,R,put):
    for j in range(4):
        for t in range(8):
            if R==64:
                f=[piece(4*t+j//2),piece(4*t+2+j//2)]
                half=lane(f[0].shape)<64
                v=jnp.where(half,f[0],pltpu.roll(f[1],64,1)) if j%2==0 else jnp.where(half,pltpu.roll(f[0],64,1),f[1])
            else:
                v=None
                for i in range(4):
                    x=piece(4*t+i); sh=(32*i-32*j)%128
                    x=pltpu.roll(x,sh,1) if sh else x
                    ln=lane(x.shape)
                    v=x if v is None else jnp.where((ln>=32*i)&(ln<32*i+32),x,v)
            put(j,t,v)
def forward_kernel(A,B,sem_names,*refs):
    ins=refs[:13]; outs=refs[13:26]; own=refs[26:39]; rest=refs[39:]
    (x_ref,og_ref,sr_ref,gain_ref,shift_ref,ob_ref,bq_ref,bfc_ref,ad_ref,wq_ref,wo_ref,wf_ref,wp_ref)=own
    (u_ref,qkv_out,o_out,lse_out,r_out,kl_out,h1_out,at_out,uu_out,bo_out,dx2_out,do_out,_)=outs
    (l_ref,h1_ref,qkv_ref,o_ref,x2_ref,h2_ref,y_ref,dh_ref,kl_ref,ql_ref,wb_ref,wout_ref,bo_ref,do_ref,lse_ref,r_ref,at_ref,uu_ref,b3_ref,bf_ref,
     isem,wsem,osem)=rest[:23]
    sems=rest[23:]
    G_=Gather(A,B,l_ref,u_ref,dict(zip(sem_names,sems)))
    R=wq_ref.shape[0]
    cin=[pltpu.make_async_copy(a,b,isem.at[i]) for i,(a,b) in enumerate(zip(ins,own))]
    X,OG,SR,GN,SH,OB,BQ,BF_,AD,WQ,WO,WF,WP=range(13)
    for i in (WQ,X,GN,SH,AD,WO,WP,WF,SR,BQ,BF_,OB,OG): cin[i].start()
    G_.greet()
    cin[WQ].wait()
    for p in range(8):
        for i in range(3):
            c0=384*p+128*i
            l_ref[c0//1024,:,c0%1024:c0%1024+128]=wq_ref[:,1024*i+128*p:1024*i+128*p+128]
    G_.greeted()
    for g in range(LEAD): G_.stage(0,jnp.int32(g))
    G_.own(0,3,0).start()
    for i in (X,GN,SH,AD): cin[i].wait()
    a=[ad_ref[i].astype(BF).astype(F32) for i in range(4)]
    z=jnp.zeros((4,D),F32)
    at_ref[...]=jnp.concatenate([a[0],a[0],a[2],a[2]],0).astype(BF)
    uq=jnp.concatenate([8.0*a[1],z,z,z],0).astype(BF); uv=jnp.concatenate([z,z,8.0*a[3],z],0).astype(BF)
    for p in range(8):
        uu_ref[:,384*p:384*p+128]=uq[:,128*p:128*p+128]
        uu_ref[:,384*p+128:384*p+256]=jnp.zeros((16,128),BF)
        uu_ref[:,384*p+256:384*p+384]=uv[:,128*p:128*p+128]
    def ln0(i,_):
        sl=pl.ds(pl.multiple_of(i*256,256),256)
        c,rs=stats(x_ref[sl,:].astype(F32))
        h1_ref[sl,:]=(c*rs*gain_ref[0:1,:]+shift_ref[0:1,:]).astype(BF)
        r_ref[sl,:]=nt(h1_ref[sl,:],at_ref[...]).astype(BF)
        return 0
    lax.fori_loop(0,2,ln0,0)
    G_.own(0,3,0).wait()
    G_.tick(0)
    for i in (WO,WP,WF,SR,BQ,BF_,OB,OG): cin[i].wait()
    l_ref[3]=wo_ref[...]
    for j in range(4): l_ref[5+2*j]=wp_ref[R*j:R*j+R,:]
    def put_w(j,t,v): l_ref[4+2*j,:,128*t:128*t+128]=v.astype(BF)
    spread(lambda k: wf_ref[:,128*k:128*k+128].astype(F32),R,put_w)
    G_.own(3,NU,1).start()
    G_.tick(1)
    lax.fori_loop(2,4,ln0,0)
    G_.tick(2)
    def put_b(j,t,v): bf_ref[j:j+1,128*t:128*t+128]=v[0:1]
    spread(lambda k: jnp.broadcast_to(bfc_ref[k:k+1,:],(8,128)),R,put_b)
    for p in range(8):
        for i in range(3): b3_ref[:,384*p+128*i:384*p+128*i+128]=bq_ref[8*i+p:8*i+p+1,:]
    e8=lane((8,128))==row((8,128))
    s_row=jnp.sum(jnp.where(e8,jnp.broadcast_to(sr_ref[:,0:1],(8,128)),0),axis=0,keepdims=True)
    kl_ref[...]=key_lanes(s_row)
    ql_ref[...]=query_lanes(None)
    lse_ref[...]=jnp.zeros((T,128),F32)
    G_.own(3,NU,1).wait()
    G_.tick(3); G_.stage(3,jnp.int32(0)); G_.tick(4); G_.stage(3,jnp.int32(1))
    def load(u,slot): return pltpu.make_async_copy(u_ref.at[u],wb_ref.at[slot],wsem.at[slot])
    def w(slot): return wb_ref[slot].reshape(D,D)
    def out(src,dst,k):
        cp=pltpu.make_async_copy(src,dst,osem.at[k]); cp.start(); return cp
    pend=[out(r_ref,r_out,14),out(kl_ref,kl_out,15),out(h1_ref,h1_out,16),out(at_ref,at_out,17),out(uu_ref,uu_out,18)]
    G_.ready(0); load(0,0).start()
    wo_cp=pltpu.make_async_copy(u_ref.at[3],wout_ref,wsem.at[4])
    def pair(p,_):
        nu=jnp.where(p>=5,2,jnp.where(p>=2,1,0))
        @pl.when((p==0)|(p==2)|(p==5))
        def _():
            load(nu,nu).wait()
            cs=pl.ds(pl.multiple_of(nu*1024,1024),1024)
            def mix(i,_):
                sl=pl.ds(pl.multiple_of(i*256,256),256)
                qkv_ref[sl,cs]=(nn(h1_ref[sl,:],w(nu))+(nn(r_ref[sl,:],uu_ref[:,cs])+b3_ref[:,cs])).astype(BF)
                return 0
            lax.fori_loop(0,4,mix,0)
            G_.tick(5+p+nu,True,2)
        qs=pl.ds(pl.multiple_of(p*384,128),128); ks=pl.ds(pl.multiple_of(p*384+128,128),128); vs=pl.ds(pl.multiple_of(p*384+256,128),128)
        oc=pl.ds(pl.multiple_of(p*128,128),128)
        lq=lane((QB,128))
        for h in range(2):
            q8=qkv_ref[:,qs]*jnp.asarray(0.125,BF)
            def put(i,o,ls,h=h):
                sl=slice(i*QB,(i+1)*QB)
                if h==0: o_ref[sl,oc]=o.astype(BF)
                else: o_ref[sl,oc]=jnp.where(lq<64,o_ref[sl,oc],o.astype(BF))
                lse_ref[sl,:]=jnp.where(lq==2*p+h,ls,lse_ref[sl,:])
            attn_fwd_head(q8,qkv_ref[:,ks],qkv_ref[:,vs],kl_ref[...],ql_ref[...],h,put)
        G_.tick(6+p+nu,True,2)
        @pl.when((p==1)|(p==3))
        def _(): G_.ready(nu+1); load(nu+1,nu+1).start()
        @pl.when(p==6)
        def _(): G_.ready(3); wo_cp.start()
        return 0
    lax.fori_loop(0,8,pair,0)
    t=16
    pend+=[out(qkv_ref,qkv_out,0),out(o_ref,o_out,1),out(lse_ref,lse_out,19)]
    wo_cp.wait()
    RB=256
    def mid0(i,_):
        sl=pl.ds(pl.multiple_of(i*RB,RB),RB)
        x2=x_ref[sl,:].astype(F32)+nn(o_ref[sl,:],wout_ref[...].reshape(D,D))+ob_ref[0:1,:]
        x2_ref[sl,:]=x2
        c,rs=stats(x2)
        h2_ref[sl,:]=(c*rs*gain_ref[1:2,:]+shift_ref[1:2,:]).astype(BF)
        y_ref[sl,:]=x2+ob_ref[1:2,:]
        dh_ref[sl,:]=jnp.zeros((RB,D),F32)
        return 0
    lax.fori_loop(0,T//RB-1,mid0,0)
    G_.ready(4); load(4,0).start()
    lax.fori_loop(T//RB-1,T//RB,mid0,0)
    G_.tick(t); t+=1
    G_.ready(5); load(5,1).start()
    base=t
    def chunk(j,_):
        s0=2*lax.rem(j,2); s1=s0+1
        load(4+2*j,s0).wait(); load(5+2*j,s1).wait()
        def blk(i,_):
            sl=pl.ds(pl.multiple_of(i*RB,RB),RB)
            wf=wb_ref[s0].reshape(D,D); wp=wb_ref[s1].reshape(D,D)
            f=nn(h2_ref[sl,:],wf)+bf_ref[pl.ds(j,1),:]
            f2=f*f
            th=jnp.tanh(C0*(f+C1*(f2*f)))
            hp=0.5*(1.0+th)
            g=(f*hp).astype(BF)
            gp=hp+(0.5*C0)*f*(1.0-th*th)*(1.0+(3*C1)*f2)
            y_ref[sl,:]+=nn(g,wp)
            dg=nt(og_ref[sl,:],wp)
            df=(dg*gp).astype(BF)
            dh_ref[sl,:]+=nt(df,wf)
            G_.tick(base+4*j+i)
            @pl.when((i==2)&(j<3))
            def _():
                G_.ready(6+2*j); load(6+2*j,2-s0).start(); G_.ready(7+2*j); load(7+2*j,3-s0).start()
            return 0
        lax.fori_loop(0,T//RB,blk,0)
        return 0
    lax.fori_loop(0,4,chunk,0)
    def last(i,_):
        sl=pl.ds(pl.multiple_of(i*RB,RB),RB)
        bo_ref[sl,:]=y_ref[sl,:].astype(BF)
        c,rs=stats(x2_ref[sl,:])
        xh=c*rs
        dy=dh_ref[sl,:]*gain_ref[1:2,:]
        dx2=og_ref[sl,:].astype(F32)+rs*(dy-jnp.mean(dy,axis=-1,keepdims=True)-xh*jnp.mean(dy*xh,axis=-1,keepdims=True))
        x2_ref[sl,:]=dx2
        do_ref[sl,:]=nt(dx2.astype(BF),wout_ref[...].reshape(D,D)).astype(BF)
        for k,(a,b) in enumerate(((bo_ref,bo_out),(x2_ref,dx2_out),(do_ref,do_out))):
            pltpu.make_async_copy(a.at[sl],b.at[sl],osem.at[2+3*i+k]).start()
        return 0
    lax.fori_loop(0,T//RB,last,0)
    for i in range(T//RB):
        sl=slice(i*RB,(i+1)*RB)
        for k,(a,b) in enumerate(((bo_ref,bo_out),(x2_ref,dx2_out),(do_ref,do_out))):
            pend.append(pltpu.make_async_copy(a.at[sl],b.at[sl],osem.at[2+3*i+k]))
    G_.finish()
    for cp in pend: cp.wait()
def forward_call(A,B,*ins):
    R=ins[9].shape[0]
    sems=Gather.sems(A,B)
    hbm=pl.BlockSpec(memory_space=pl.ANY)
    sd=jax.ShapeDtypeStruct; V=pltpu.VMEM
    outs=[sd((NU,A,B,2,R,D),BF),sd((T,3*D),BF),sd((T,D),BF),sd((T,128),F32),sd((T,16),BF),sd((T,128),BF),sd((T,D),BF),sd((16,D),BF),sd((16,3*D),BF),
          sd((T,D),BF),sd((T,D),F32),sd((T,D),BF)]
    def kernel(*refs):
        forward_kernel(A,B,list(sems),*refs[:25],None,*refs[25:])
    return pl.pallas_call(kernel,in_specs=[hbm]*13,out_specs=[hbm]*12,out_shape=outs,
      scratch_shapes=[V(v.shape,v.dtype) for v in ins]+[V((NU,R,D),BF),V((T,D),BF),V((T,3*D),BF),V((T,D),BF),V((T,D),F32),V((T,D),BF),
        V((T,D),F32),V((T,D),F32),V((T,128),BF),V((T,128),BF),V((4,A,B,2,R,D),BF),V((A,B,2,R,D),BF),V((T,D),BF),V((T,D),BF),V((T,128),F32),V((T,16),BF),
        V((16,D),BF),V((16,3*D),BF),V((1,3*D),F32),V((4,D),F32),
        pltpu.SemaphoreType.DMA((13,)),pltpu.SemaphoreType.DMA((5,)),pltpu.SemaphoreType.DMA((20,))]+list(sems.values()),
      compiler_params=pltpu.CompilerParams(collective_id=0,has_side_effects=True,vmem_limit_bytes=61*2**20),name="front")(*ins)

def back_kernel(kl_in,uu_in,r_in,lse_in,h1_in,qkv_ref,do_ref,o_ref,bo_in,dm_ref,drb_ref,ga_ref,bo_ref,
                kl_ref,uu_ref,r_ref,lse_ref,h1_ref,dr_ref,gs_ref,sem):
    p=pl.program_id(0)
    cps=[pltpu.make_async_copy(a,b,sem.at[i]) for i,(a,b) in enumerate(zip((lse_in,kl_in,uu_in,r_in,h1_in),(lse_ref,kl_ref,uu_ref,r_ref,h1_ref)))]
    @pl.when(p==0)
    def _():
        for cp in cps: cp.start()
        for cp in cps[:4]: cp.wait()
        dr_ref[...]=jnp.zeros((T,16),F32)
    bo_ref[...]=bo_in[...]
    l=lane((T,128))
    lse=lse_ref[...]
    lc=[jnp.sum(jnp.where(l==2*p+h,lse,0.0),axis=1,keepdims=True) for h in range(2)]
    def store(kind,sl,val):
        o={"q":0,"k":128,"v":256}[kind]
        dm_ref[sl,o:o+128]=val.astype(BF)
    attn_bwd_pair(qkv_ref[:,0:128],qkv_ref[:,128:256],qkv_ref[:,256:384],do_ref[...],o_ref[...],lc,kl_ref[...],store)
    dmp=dm_ref[...]
    dr_ref[...]+=nt(dmp,uu_ref[:,pl.ds(pl.multiple_of(p*384,128),384)])
    gu=tn(r_ref[...],dmp)*8.0
    oc=pl.ds(pl.multiple_of(p*128,128),128)
    ga_ref[1,:,oc]=gu[4:8,0:128]
    ga_ref[3,:,oc]=gu[12:16,256:384]
    @pl.when(p==7)
    def _():
        cps[4].wait()
        drb=dr_ref[...].astype(BF)
        drb_ref[...]=drb
        gs_ref[...]=tn(drb,h1_ref[...])
        ga_ref[0]=gs_ref[0:4,:]
        ga_ref[2]=gs_ref[8:12,:]
def back_call(kl,uu,r,lse,h1,qkv,do,o,bo):
    pb=lambda wd: pl.BlockSpec((T,wd),lambda p:(0,p))
    sd=jax.ShapeDtypeStruct; V=pltpu.VMEM
    hbm=pl.BlockSpec(memory_space=pl.ANY)
    first=(kl,uu,r,lse,h1)
    return pl.pallas_call(back_kernel,grid=(8,),
      in_specs=[hbm]*5+[pb(384),pb(128),pb(128),pb(128)],
      out_specs=[pb(384),VM,VM,pb(128)],
      out_shape=[sd((T,3*D),BF),sd((T,16),BF),sd((4,4,D),F32),sd((T,D),BF)],
      scratch_shapes=[V(v.shape,v.dtype) for v in first]+[V((T,16),F32),V((16,D),F32),pltpu.SemaphoreType.DMA((5,))],
      compiler_params=pltpu.CompilerParams(vmem_limit_bytes=60*2**20),name="back")(*first,qkv,do,o,bo)

def sum_kernel(A,B,DP,ga_in,x_in,gain_in,u_in,at_in,drb_in,dx2_in,dm_in,o_ref,ig_out,
               g_ref,x_ref,gain_ref,w_ref,at_ref,drb_ref,dx2_ref,dm_ref,c_ref,h_ref,b_ref,z_ref,t_ref,ss,rs,sem,osem):
    ins=(ga_in,gain_in,at_in,drb_in,u_in.at[0:3],dm_in,x_in,dx2_in)
    own=(g_ref,gain_ref,at_ref,drb_ref,w_ref,dm_ref,x_ref,dx2_ref)
    cin=[pltpu.make_async_copy(p,q,sem.at[i]) for i,(p,q) in enumerate(zip(ins[:5],own[:5]))]
    def part(k,i):
        sl=pl.ds(pl.multiple_of(i*256,256),256)
        return pltpu.make_async_copy(ins[k].at[sl],own[k].at[sl],sem.at[5+3*i+k-5])
    for cp in cin: cp.start()
    for i in range(4):
        for k in (5,6,7): part(k,i).start()
    def block(i):
        for k in (5,6,7): part(k,i).wait()
        sl=pl.ds(pl.multiple_of(i*256,256),256)
        dm=dm_ref[sl,:]
        dh=nn(drb_ref[sl,:],at_ref[...])
        for u in range(3): dh=dh+nt(dm[:,u*1024:u*1024+1024],w_ref[u].reshape(D,D))
        v,s=stats(x_ref[sl,:].astype(F32))
        xh=v*s
        dy=dh*gain_ref[0:1,:]
        dx2_ref[sl,:]=dx2_ref[sl,:]+s*(dy-jnp.mean(dy,axis=-1,keepdims=True)-xh*jnp.mean(dy*xh,axis=-1,keepdims=True))
        pltpu.make_async_copy(dx2_ref.at[sl],ig_out.at[sl],osem.at[i]).start()
    f=lax.axis_index("fsdp"); d=lax.axis_index("dp")
    c=f&1; h=f>>1; b=h&(B-1); a=h>>(B.bit_length()-1)
    def dev(a,b,c,e): return {"fsdp":(a*B+b)*2+c,"dp":e}
    L1,L2=(A,B) if A>=B else (B,A)
    m1,m2=(a,b) if A>=B else (b,a)
    at=(lambda p,q: (p,q)) if A>=B else (lambda p,q: (q,p))
    nb=DP*L2
    me=d*L2+m2
    sib=dev(a,b,1-c,d)
    near=[]
    for k in range(1,nb):
        o=(me+k)&(nb-1)
        near.append(dev(*at(m1,o&(L2-1)),c,o>>(L2.bit_length()-1)))
    far=[dev(*at((m1+k)&(L1-1),m2),c,d) for k in range(1,L1)]
    bar=pltpu.get_barrier_semaphore()
    for p in [sib]+near+far: pl.semaphore_signal(bar,inc=1,device_id=p,device_id_type=MESH)
    pl.semaphore_wait(bar,1+len(near)+len(far))
    def rc(src,dst,k,to): return pltpu.make_async_remote_copy(src_ref=src,dst_ref=dst,send_sem=ss.at[k],recv_sem=rs.at[k],device_id=to,device_id_type=MESH)
    cin[0].wait()
    cps=[rc(g_ref.at[pl.ds(2*(1-c),2)],c_ref,0,sib)]
    cps[0].start()
    for cp in cin[1:]: cp.wait()
    cps[0].wait_recv()
    h_ref[...]=g_ref[pl.ds(2*c,2)]+c_ref[...]
    b_ref[me]=h_ref[...]
    first=[rc(h_ref,b_ref.at[me],k,to) for k,to in enumerate(near,1)]
    for cp in first: cp.start()
    lax.fori_loop(0,1,lambda i,_: (block(i),0)[1],0)
    for cp in first: cp.wait_recv()
    v=b_ref[0]
    for k in range(1,nb): v=v+b_ref[k]
    t_ref[...]=v
    z_ref[m1]=v
    second=[rc(t_ref,z_ref.at[m1],k,to) for k,to in enumerate(far,nb)]
    for cp in second: cp.start()
    lax.fori_loop(1,3,lambda i,_: (block(i),0)[1],0)
    for cp in second: cp.wait_recv()
    v=z_ref[0]
    for k in range(1,L1): v=v+z_ref[k]
    half=o_ref.at[pl.ds(2*c,2)]
    o_ref[pl.ds(2*c,2)]=v
    back=rc(half,half,nb+L1-1,sib)
    back.start()
    lax.fori_loop(3,4,lambda i,_: (block(i),0)[1],0)
    back.wait_recv()
    for cp in cps+first+second+[back]: cp.wait_send()
    for i in range(4):
        sl=slice(i*256,i*256+256)
        pltpu.make_async_copy(dx2_ref.at[sl],ig_out.at[sl],osem.at[i]).wait()
def sum_call(A,B,DP,*ins):
    g=ins[0]
    L1,L2=max(A,B),min(A,B); nb=DP*L2; n=nb+L1
    V=pltpu.VMEM; hs=(2,)+g.shape[1:]
    hbm=pl.BlockSpec(memory_space=pl.ANY)
    sems=pltpu.SemaphoreType.DMA
    return pl.pallas_call(functools.partial(sum_kernel,A,B,DP),in_specs=[hbm]*8,out_specs=[VM,hbm],
      out_shape=[jax.ShapeDtypeStruct(g.shape,F32),jax.ShapeDtypeStruct((T,D),F32)],
      scratch_shapes=[V((3,)+v.shape[1:],v.dtype) if k==3 else V(v.shape,v.dtype) for k,v in enumerate(ins)]+[V(hs,F32),V(hs,F32),V((nb,)+hs,F32),V((L1,)+hs,F32),V(hs,F32),
        sems((n,)),sems((n,)),sems((17,)),sems((4,))],
      compiler_params=pltpu.CompilerParams(collective_id=1,has_side_effects=True,vmem_limit_bytes=61*2**20),name="total")(*ins)

def update_kernel(rate,g_in,m_in,a_in,v_in,ig_in,g_out,m_out,a_out,v_out,c_out,ig_out,g_ref,m_ref,a_ref,v_ref,c_ref,ig_ref,isem,osem):
    small=[pltpu.make_async_copy(p,q,isem.at[i]) for i,(p,q) in enumerate(((g_in,g_ref),(m_in,m_ref),(a_in,a_ref),(v_in,v_ref)))]
    for cp in small: cp.start()
    n=ig_ref.shape[0]//4
    rin=[pltpu.make_async_copy(ig_in.at[i*n:i*n+n],ig_ref.at[i*n:i*n+n],isem.at[4+i]) for i in range(4)]
    rout=[pltpu.make_async_copy(ig_ref.at[i*n:i*n+n],ig_out.at[i*n:i*n+n],osem.at[5+i]) for i in range(4)]
    for cp in rin: cp.start()
    for cp in small: cp.wait()
    g=g_ref[...]
    mom=0.9*m_ref[...]+g
    new=a_ref[...]-rate*(g+0.9*mom)
    m_ref[...]=mom
    a_ref[...]=new
    v_ref[...]=0.9*v_ref[...]+0.1*new
    c_ref[...]=new.astype(BF)
    outs=[pltpu.make_async_copy(p,q,osem.at[i]) for i,(p,q) in enumerate(((g_ref,g_out),(m_ref,m_out),(a_ref,a_out),(v_ref,v_out),(c_ref,c_out)))]
    for cp in outs: cp.start()
    for i in range(4): rin[i].wait(); rout[i].start()
    for cp in outs+rout: cp.wait()
def update_call(rate,g,m,a,v,ig):
    hbm=pl.BlockSpec(memory_space=pl.ANY)
    sd=jax.ShapeDtypeStruct; V=pltpu.VMEM
    return pl.pallas_call(functools.partial(update_kernel,rate),in_specs=[hbm]*5,out_specs=[hbm]*6,
      out_shape=[sd(g.shape,F32)]*4+[sd(g.shape,BF),sd(ig.shape,F32)],
      scratch_shapes=[V(g.shape,F32)]*4+[V(g.shape,BF),V(ig.shape,F32),pltpu.SemaphoreType.DMA((8,)),pltpu.SemaphoreType.DMA((9,))],
      compiler_params=pltpu.CompilerParams(vmem_limit_bytes=61*2**20),name="update")(g,m,a,v,ig)
def solution(mesh):
    F=mesh.shape["fsdp"]; DP=mesh.shape["dp"]
    A,B=(F//4,2) if F<=16 else (2,F//4)
    def per_device(tokens,item_start,og,gains,shifts,wqkv,bqkv,wout,wfc,bfc,wproj,ob,adapters,momentum,average):
        u,qkv,o,lse,r,kl,h1,at,uu,bo,dx2,do=forward_call(A,B,tokens,og,item_start.reshape(8,128),gains,shifts,ob,bqkv.reshape(24,128),bfc.reshape(32,128),
            adapters.transpose(0,2,1),wqkv,wout,wfc,wproj)
        dm,drb,ga,bo=back_call(kl,uu,r,lse,h1,qkv,do,o,bo)
        grad,ig=sum_call(A,B,DP,ga,tokens,gains,u,at,drb,dx2,dm)
        t=lambda v: v.transpose(0,2,1)
        rate=0.01/math.sqrt(tokens.shape[0]*F*DP)
        grad,mom,new,avg,low,ig=update_call(rate,grad,t(momentum),t(adapters),t(average),ig)
        return bo,ig,t(grad),t(mom),t(new),t(avg),t(low)
    rows=P(("fsdp","dp"),None); w=P("fsdp",None); n=P()
    return jax.shard_map(per_device,mesh=mesh,
      in_specs=(rows,P(("fsdp","dp")),rows,n,n,w,n,w,w,n,w,n,n,n,n),out_specs=(rows,rows,n,n,n,n,n),check_vma=False)
```

profile of v0, /device:TPU:0, one launch (start us, length us, event | category | flops | bytes accessed | tf_op | source)
XLA Modules:
  0.0 209.9 jit_solution(6108998595016930114)
XLA Ops:
  0.6 141.3 %front.1 = (bf16[12,4,2,2,64,1024]{5,4,3,2,1,0:T(8,128)(2,1)}, bf16[1024,3072]{1,0:T(8,128)(2,1)}, bf16[1024,1024]{1,0:T(8,128)(2,1)}, f32[1024,128]{1,0:T(8,128...) custom-call(bf16[1024,1024]{1,0:T(8,128)(2,1)} %x_in.1, ...), custom_call_target="tpu_custom_call" | custom-call | tf_op jit(solution)/shard_map/front/pallas_call | solution.py:365
  142.0 45.8 %back.1 = (bf16[1024,3072]{1,0:T(8,128)(2,1)}, bf16[1024,16]{1,0:T(8,128)(2,1)}, f32[4,4,1024]{2,1,0:T(4,128)}, bf16[1024,1024]{1,0:T(8,128)(2,1)}) custom-call(bf16[1024,128]{1,0:T(8,128)(2,1)} %get-tuple-element.31.kl_in, bf16[16,3072]{1,0:T(8,128)(2,1)} %get-tuple-element.32.uu_in, bf16[1024,16]{1,0:T(8,128)(2,1)} %get-tuple-element.33.r_in, ...), custom_call_target="tpu_custom_call" | custom-call | tf_op jit(solution)/shard_map/back/pallas_call | solution.py:408
  187.8 18.1 %total.1 = (f32[4,4,1024]{2,1,0:T(4,128)}, f32[1024,1024]{1,0:T(8,128)}) custom-call(f32[4,4,1024]{2,1,0:T(4,128)} %get-tuple-element.41.ga_in, bf16[1024,1024]{1,0:T(8,128)(2,1)} %x_in.1, f32[2,1024]{1,0:T(2,128)} %gain_in.1, bf16[12,4,2,2,64,1024]{5,4,3,2,1,0:T(8,128)(2,1)} %get-tuple-element.42.u_in, bf16[16,1024]{1,0:T(8,128)(2,1)} %get-tuple-element.43.at_in, ...), custom_call_target="tpu_custom_call" | custom-call | tf_op jit(solution)/shard_map/total/pallas_call | solution.py:492
  205.9 3.8 %update.1 = (f32[4,4,1024]{2,1,0:T(4,128)}, f32[4,4,1024]{2,1,0:T(4,128)}, f32[4,4,1024]{2,1,0:T(4,128)}, f32[4,4,1024]{2,1,0:T(4,128)}, bf16[4,4,1024]{2,1,0:T(4,128)(2,1)}, /*index=5*/f32[1024,1024]{1,0:T(8,128)}) custom-call(f32[4,4,1024]{2,1,0:T(4,128)} %get-tuple-element.47.g_in, f32[4,4,1024]{2,1,0:T(4,128)} %bitcast.13, f32[4,4,1024]{2,1,0:T(4,128)} %bitcast.12, ...), custom_call_target="tpu_custom_call" | custom-call | tf_op jit(solution)/shard_map/update/pallas_call | solution.py:520
where the time goes:
time: 210 us
  Pallas kernels  209 us (100%)
    pallas_call x1, Pallas kernels, forward_call(): pl.pallas_call(kernel, in_specs=[hbm] * 13, out_specs=[hbm] * 12, out_sha...  141 us
    pallas_call x1, Pallas kernels, back_call(): pl.pallas_call(back_kernel, grid=(8,), in_specs=[hbm] * 5 + [pb(384), pb(...  45.8 us
    pallas_call x1, Pallas kernels, sum_call(): pl.pallas_call(functools.partial(sum_kernel, A, B, DP), in_specs=[hbm] *...  18.1 us

commit v1 on v0

--- a/solution.py
+++ b/solution.py
@@ -73,7 +73,7 @@
         store("v",sl,jnp.where(lk,res[0][2][i],res[1][2][i]))
 MESH=pl.DeviceIdType.MESH
 
-NU=12; NC=24; LEAD=3; OFFS=(-LEAD,0,2,4); XC=384
+NU=12; NC=24; LEAD=4; OFFS=(-LEAD,0,2,4,-1); XC=384
 class Gather:
     def __init__(self,A,B,l_ref,u_ref,S):
         self.l,self.u,self.S=l_ref,u_ref,S
@@ -86,8 +86,14 @@
         def along_a(k): return (self.a+k)&(A-1),self.b
         def along_b(k): return self.a,(self.b+k)&(B-1)
         l1,l2=(along_a,along_b) if self.long_a else (along_b,along_a)
+        self.relay=self.L1==4
+        q=self.a if self.long_a else self.b
+        self.end=(q==0)|(q==3); self.mid=(q==1)|(q==2); self.q=q
         self.p1=[l1(k) for k in range(1,self.L1)]; self.p2=[l2(k) for k in range(1,self.L2)]
         self.d1=[dev(*p,self.c,d) for p in self.p1]; self.d2=[dev(*p,self.c,d) for p in self.p2]
+        hop=jnp.where(q==1,0,jnp.where(q==2,3,q)) if self.relay else q
+        self.dq=dev(hop,self.b,self.c,d) if self.long_a else dev(self.a,hop,self.c,d)
+        self.far=self.p1[1] if self.relay else None
         self.dx=dev(self.a,self.b,self.c,d+1-2*par); self.dc=dev(self.a,self.b,1-self.c,d)
         self.carried=pl.ds(pl.multiple_of(par*XC,128),D-XC)
         self.crossed=pl.ds(pl.multiple_of(par*(D-XC),128),XC)
@@ -121,19 +127,35 @@
     def cs(self,g):
         u,r=self.rows(g); v=self.u.at[u,:,:,self.c,r]
         return [self.rc(v,v,"c",g,self.dc)]
-    def box(self,name,u,r):
-        n1=slice(0,self.L1-1); n2=slice(0,self.L2-1); al=slice(None)
-        m={"z":(n1,0,self.carried),"y":(al,n2,self.carried),"x":(n1,0,self.crossed),"w":(al,n2,self.crossed),"c":(al,al,al)}[name]
+    def qs(self,g):
+        u,r=self.rows(g); v=self.u.at[u,self.far[0],self.far[1],self.c,r,self.carried]
+        return self.rc(v,v,"q",g,self.dq)
+    def box(self,name,u,r,n=None):
+        n1=slice(0,n or self.L1-1); n2=slice(0,self.L2-1); al=slice(None)
+        m={"z":(n1,0,self.carried),"y":(al,n2,self.carried),"x":(n1,0,self.crossed),"w":(al,n2,self.crossed),"c":(al,al,al),"q":(slice(0,1),0,self.carried)}[name]
         i1,i2=(m[0],m[1]) if self.long_a else (m[1],m[0])
         return self.u.at[u,i1,i2,0,r,m[2]]
-    def got(self,name,g):
-        u,r=self.rows(g); v=self.box(name,u,r)
+    def got(self,name,g,n=None):
+        u,r=self.rows(g); v=self.box(name,u,r,n)
         self.rc(v,v,name,g,self.dc).wait_recv()
     def stage(self,s,g):
         if s==0:
-            for cp in self.zs(g): cp.start()
+            for k,cp in enumerate(self.zs(g),1):
+                if self.relay and k!=2:
+                    @pl.when(self.q!=(3 if k==1 else 0))
+                    def _(cp=cp): cp.start()
+                else: cp.start()
+        elif s==4:
+            if not self.relay: self.got("z",g)
+            else:
+                @pl.when(self.end)
+                def _(): self.got("z",g,2)
+                @pl.when(self.mid)
+                def _(): self.got("z",g); self.qs(g).start()
         elif s==1:
-            self.got("z",g)
+            if self.relay:
+                @pl.when(self.end)
+                def _(): self.got("q",g)
             for cp in self.ys(g)+self.xs(g): cp.start()
         elif s==2:
             self.got("y",g)
@@ -142,10 +164,11 @@
             self.got("x",g); self.got("w",g)
             for cp in self.cs(g): cp.start()
     def tick(self,t,safe=False,least=0):
-        for s,o in enumerate(OFFS):
+        for s in (0,3,2,4,1):
+            o=OFFS[s]
             if isinstance(t,int):
                 if (2 if s==3 else 0)<=t-o<NC: self.stage(s,jnp.int32(t-o))
-            elif safe and s<3: self.stage(s,t-o)
+            elif safe and s!=3: self.stage(s,t-o)
             elif safe:
                 @pl.when(t-o>=least)
                 def _(s=s,o=o): self.stage(s,t-o)
@@ -155,13 +178,20 @@
     def ready(self,u):
         self.got("c",2*u); self.got("c",2*u+1)
     def finish(self):
-        for n in "zyxwc":
-            v=self.box(n,slice(None),slice(None))
+        def sent(n,k=None):
+            v=self.box(n,slice(None),slice(None),k)
             self.rc(v,v,n,0,self.dc).wait_send()
+        for n in "yxwc": sent(n)
+        if not self.relay: sent("z")
+        else:
+            @pl.when(self.end)
+            def _(): sent("z",2)
+            @pl.when(self.mid)
+            def _(): sent("z"); sent("q")
     @staticmethod
     def sems(A,B):
         s={"loc":(2,)}
-        for n in "zyxwc": s[n+"s"]=(); s[n+"r"]=(NC,)
+        for n in "zqyxwc": s[n+"s"]=(); s[n+"r"]=(NC,)
         return {n:pltpu.SemaphoreType.DMA(v) for n,v in s.items()}
 
 def attn_fwd_head(q8,k,v,klanes,qlanes,h,put):
@@ -233,6 +263,7 @@
         return 0
     lax.fori_loop(0,2,ln0,0)
     G_.own(0,3,0).wait()
+    G_.stage(4,jnp.int32(0))
     G_.tick(0)
     for i in (WO,WP,WF,SR,BQ,BF_,OB,OG): cin[i].wait()
     l_ref[3]=wo_ref[...]
@@ -327,9 +358,10 @@
             df=(dg*gp).astype(BF)
             dh_ref[sl,:]+=nt(df,wf)
             G_.tick(base+4*j+i)
+            @pl.when((i==1)&(j<3))
+            def _(): G_.ready(6+2*j); load(6+2*j,2-s0).start()
             @pl.when((i==2)&(j<3))
-            def _():
-                G_.ready(6+2*j); load(6+2*j,2-s0).start(); G_.ready(7+2*j); load(7+2*j,3-s0).start()
+            def _(): G_.ready(7+2*j); load(7+2*j,3-s0).start()
             return 0
         lax.fori_loop(0,T//RB,blk,0)
         return 0
@@ -346,7 +378,7 @@
         for k,(a,b) in enumerate(((bo_ref,bo_out),(x2_ref,dx2_out),(do_ref,do_out))):
             pltpu.make_async_copy(a.at[sl],b.at[sl],osem.at[2+3*i+k]).start()
         return 0
-    lax.fori_loop(0,T//RB,last,0)
+    lax.fori_loop(0,T//RB,last,0,unroll=2)
     for i in range(T//RB):
         sl=slice(i*RB,(i+1)*RB)
         for k,(a,b) in enumerate(((bo_ref,bo_out),(x2_ref,dx2_out),(do_ref,do_out))):

time: 210 us -> 205 us (0.976)
  Pallas kernels: 209 us -> 204 us
    pallas_call x1, Pallas kernels: 18.1 us -> 15 us  [sum_call(): pl.pallas_call(functools.partial(sum_kernel, A, B, DP), in_specs=[hbm] *...]
    pallas_call x1, Pallas kernels: 141 us -> 139 us  [forward_call(): pl.pallas_call(kernel, in_specs=[hbm] * 13, out_specs=[hbm] * 12, out_sha...]
where the time goes in v1:
time: 205 us; the launch traced here: 204 us
  Pallas kernels  204 us (100%)
    pallas_call x1, Pallas kernels, forward_call(): pl.pallas_call(kernel, in_specs=[hbm] * 13, out_specs=[hbm] * 12, out_sha...  139 us
    pallas_call x1, Pallas kernels, back_call(): pl.pallas_call(back_kernel, grid=(8,), in_specs=[hbm] * 5 + [pb(384), pb(...  45.6 us
    pallas_call x1, Pallas kernels, sum_call(): pl.pallas_call(functools.partial(sum_kernel, A, B, DP), in_specs=[hbm] *...  15 us

profile of v1, /device:TPU:0, one launch (start us, length us, event | category | flops | bytes accessed | tf_op | source)
XLA Modules:
  0.0 204.3 jit_solution(16870295122829549267)
XLA Ops:
  0.6 139.0 %front.1 = (bf16[12,4,2,2,64,1024]{5,4,3,2,1,0:T(8,128)(2,1)}, bf16[1024,3072]{1,0:T(8,128)(2,1)}, bf16[1024,1024]{1,0:T(8,128)(2,1)}, f32[1024,128]{1,0:T(8,128...) custom-call(bf16[1024,1024]{1,0:T(8,128)(2,1)} %x_in.1, ...), custom_call_target="tpu_custom_call" | custom-call | tf_op jit(solution)/shard_map/front/pallas_call | solution.py:397
  139.7 45.6 %back.1 = (bf16[1024,3072]{1,0:T(8,128)(2,1)}, bf16[1024,16]{1,0:T(8,128)(2,1)}, f32[4,4,1024]{2,1,0:T(4,128)}, bf16[1024,1024]{1,0:T(8,128)(2,1)}) custom-call(bf16[1024,128]{1,0:T(8,128)(2,1)} %get-tuple-element.31.kl_in, bf16[16,3072]{1,0:T(8,128)(2,1)} %get-tuple-element.32.uu_in, bf16[1024,16]{1,0:T(8,128)(2,1)} %get-tuple-element.33.r_in, ...), custom_call_target="tpu_custom_call" | custom-call | tf_op jit(solution)/shard_map/back/pallas_call | solution.py:440
  185.3 15.0 %total.1 = (f32[4,4,1024]{2,1,0:T(4,128)}, f32[1024,1024]{1,0:T(8,128)}) custom-call(f32[4,4,1024]{2,1,0:T(4,128)} %get-tuple-element.41.ga_in, bf16[1024,1024]{1,0:T(8,128)(2,1)} %x_in.1, f32[2,1024]{1,0:T(2,128)} %gain_in.1, bf16[12,4,2,2,64,1024]{5,4,3,2,1,0:T(8,128)(2,1)} %get-tuple-element.42.u_in, bf16[16,1024]{1,0:T(8,128)(2,1)} %get-tuple-element.43.at_in, ...), custom_call_target="tpu_custom_call" | custom-call | tf_op jit(solution)/shard_map/total/pallas_call | solution.py:524
  200.4 3.8 %update.1 = (f32[4,4,1024]{2,1,0:T(4,128)}, f32[4,4,1024]{2,1,0:T(4,128)}, f32[4,4,1024]{2,1,0:T(4,128)}, f32[4,4,1024]{2,1,0:T(4,128)}, bf16[4,4,1024]{2,1,0:T(4,128)(2,1)}, /*index=5*/f32[1024,1024]{1,0:T(8,128)}) custom-call(f32[4,4,1024]{2,1,0:T(4,128)} %get-tuple-element.47.g_in, f32[4,4,1024]{2,1,0:T(4,128)} %bitcast.13, f32[4,4,1024]{2,1,0:T(4,128)} %bitcast.12, ...), custom_call_target="tpu_custom_call" | custom-call | tf_op jit(solution)/shard_map/update/pallas_call | solution.py:552

commit v2 on v1

--- a/solution.py
+++ b/solution.py
@@ -30,10 +30,10 @@
         hi,mid,lo=cols
         base=jnp.where(l==8,hi,jnp.where(l==9,mid,jnp.where(l==10,lo,base)))
     return base.astype(BF)
-QB=256
+QB=512
 VM=pl.BlockSpec(memory_space=pltpu.VMEM)
 C0=0.7978845608; C1=0.044715
-def attn_bwd_pair(q,k,v,do,o,lcols,klanes,store,KB=256):
+def attn_bwd_pair(q,k,v,do,o,lcols,klanes,store,KB=512):
     l=lane((T,128))
     q8=q*jnp.asarray(0.125,BF)
     ka=jnp.concatenate([k,klanes],axis=1)

time: 205 us -> 202 us (0.985)
  Pallas kernels: 204 us -> 201 us
    pallas_call x1, Pallas kernels: 139 us -> 137 us  [forward_call(): pl.pallas_call(kernel, in_specs=[hbm] * 13, out_specs=[hbm] * 12, out_sha...]
where the time goes in v2:
time: 202 us
  Pallas kernels  201 us (100%)
    pallas_call x1, Pallas kernels, forward_call(): pl.pallas_call(kernel, in_specs=[hbm] * 13, out_specs=[hbm] * 12, out_sha...  137 us
    pallas_call x1, Pallas kernels, back_call(): pl.pallas_call(back_kernel, grid=(8,), in_specs=[hbm] * 5 + [pb(384), pb(...  44.4 us
    pallas_call x1, Pallas kernels, sum_call(): pl.pallas_call(functools.partial(sum_kernel, A, B, DP), in_specs=[hbm] *...  16 us

profile of v2, /device:TPU:0, one launch (start us, length us, event | category | flops | bytes accessed | tf_op | source)
XLA Modules:
  0.0 201.7 jit_solution(17351708072392918461)
XLA Ops:
  0.6 136.7 %front.1 = (bf16[12,4,2,2,64,1024]{5,4,3,2,1,0:T(8,128)(2,1)}, bf16[1024,3072]{1,0:T(8,128)(2,1)}, bf16[1024,1024]{1,0:T(8,128)(2,1)}, f32[1024,128]{1,0:T(8,128...) custom-call(bf16[1024,1024]{1,0:T(8,128)(2,1)} %x_in.1, ...), custom_call_target="tpu_custom_call" | custom-call | tf_op jit(solution)/shard_map/front/pallas_call | solution.py:397
  137.3 44.4 %back.1 = (bf16[1024,3072]{1,0:T(8,128)(2,1)}, bf16[1024,16]{1,0:T(8,128)(2,1)}, f32[4,4,1024]{2,1,0:T(4,128)}, bf16[1024,1024]{1,0:T(8,128)(2,1)}) custom-call(bf16[1024,128]{1,0:T(8,128)(2,1)} %get-tuple-element.31.kl_in, bf16[16,3072]{1,0:T(8,128)(2,1)} %get-tuple-element.32.uu_in, bf16[1024,16]{1,0:T(8,128)(2,1)} %get-tuple-element.33.r_in, ...), custom_call_target="tpu_custom_call" | custom-call | tf_op jit(solution)/shard_map/back/pallas_call | solution.py:440
  181.8 16.0 %total.1 = (f32[4,4,1024]{2,1,0:T(4,128)}, f32[1024,1024]{1,0:T(8,128)}) custom-call(f32[4,4,1024]{2,1,0:T(4,128)} %get-tuple-element.41.ga_in, bf16[1024,1024]{1,0:T(8,128)(2,1)} %x_in.1, f32[2,1024]{1,0:T(2,128)} %gain_in.1, bf16[12,4,2,2,64,1024]{5,4,3,2,1,0:T(8,128)(2,1)} %get-tuple-element.42.u_in, bf16[16,1024]{1,0:T(8,128)(2,1)} %get-tuple-element.43.at_in, ...), custom_call_target="tpu_custom_call" | custom-call | tf_op jit(solution)/shard_map/total/pallas_call | solution.py:524
  197.7 3.8 %update.1 = (f32[4,4,1024]{2,1,0:T(4,128)}, f32[4,4,1024]{2,1,0:T(4,128)}, f32[4,4,1024]{2,1,0:T(4,128)}, f32[4,4,1024]{2,1,0:T(4,128)}, bf16[4,4,1024]{2,1,0:T(4,128)(2,1)}, /*index=5*/f32[1024,1024]{1,0:T(8,128)}) custom-call(f32[4,4,1024]{2,1,0:T(4,128)} %get-tuple-element.47.g_in, f32[4,4,1024]{2,1,0:T(4,128)} %bitcast.13, f32[4,4,1024]{2,1,0:T(4,128)} %bitcast.12, ...), custom_call_target="tpu_custom_call" | custom-call | tf_op jit(solution)/shard_map/update/pallas_call | solution.py:552

commit v3 on v2

--- a/solution.py
+++ b/solution.py
@@ -302,7 +302,7 @@
                 sl=pl.ds(pl.multiple_of(i*256,256),256)
                 qkv_ref[sl,cs]=(nn(h1_ref[sl,:],w(nu))+(nn(r_ref[sl,:],uu_ref[:,cs])+b3_ref[:,cs])).astype(BF)
                 return 0
-            lax.fori_loop(0,4,mix,0)
+            lax.fori_loop(0,4,mix,0,unroll=2)
             G_.tick(5+p+nu,True,2)
         qs=pl.ds(pl.multiple_of(p*384,128),128); ks=pl.ds(pl.multiple_of(p*384+128,128),128); vs=pl.ds(pl.multiple_of(p*384+256,128),128)
         oc=pl.ds(pl.multiple_of(p*128,128),128)

time: 202 us -> 202 us (level)
  no operation moved by 1% of the time
where the time goes in v3:
time: 202 us; the launch traced here: 201 us
  Pallas kernels  201 us (100%)
    pallas_call x1, Pallas kernels, forward_call(): pl.pallas_call(kernel, in_specs=[hbm] * 13, out_specs=[hbm] * 12, out_sha...  136 us
    pallas_call x1, Pallas kernels, back_call(): pl.pallas_call(back_kernel, grid=(8,), in_specs=[hbm] * 5 + [pb(384), pb(...  44.4 us
    pallas_call x1, Pallas kernels, sum_call(): pl.pallas_call(functools.partial(sum_kernel, A, B, DP), in_specs=[hbm] *...  16.1 us

profile of v3, /device:TPU:0, one launch (start us, length us, event | category | flops | bytes accessed | tf_op | source)
XLA Modules:
  0.0 201.4 jit_solution(10274700818828274282)
XLA Ops:
  0.6 136.2 %front.1 = (bf16[12,4,2,2,64,1024]{5,4,3,2,1,0:T(8,128)(2,1)}, bf16[1024,3072]{1,0:T(8,128)(2,1)}, bf16[1024,1024]{1,0:T(8,128)(2,1)}, f32[1024,128]{1,0:T(8,128...) custom-call(bf16[1024,1024]{1,0:T(8,128)(2,1)} %x_in.1, ...), custom_call_target="tpu_custom_call" | custom-call | tf_op jit(solution)/shard_map/front/pallas_call | solution.py:397
  136.9 44.4 %back.1 = (bf16[1024,3072]{1,0:T(8,128)(2,1)}, bf16[1024,16]{1,0:T(8,128)(2,1)}, f32[4,4,1024]{2,1,0:T(4,128)}, bf16[1024,1024]{1,0:T(8,128)(2,1)}) custom-call(bf16[1024,128]{1,0:T(8,128)(2,1)} %get-tuple-element.31.kl_in, bf16[16,3072]{1,0:T(8,128)(2,1)} %get-tuple-element.32.uu_in, bf16[1024,16]{1,0:T(8,128)(2,1)} %get-tuple-element.33.r_in, ...), custom_call_target="tpu_custom_call" | custom-call | tf_op jit(solution)/shard_map/back/pallas_call | solution.py:440
  181.3 16.1 %total.1 = (f32[4,4,1024]{2,1,0:T(4,128)}, f32[1024,1024]{1,0:T(8,128)}) custom-call(f32[4,4,1024]{2,1,0:T(4,128)} %get-tuple-element.41.ga_in, bf16[1024,1024]{1,0:T(8,128)(2,1)} %x_in.1, f32[2,1024]{1,0:T(2,128)} %gain_in.1, bf16[12,4,2,2,64,1024]{5,4,3,2,1,0:T(8,128)(2,1)} %get-tuple-element.42.u_in, bf16[16,1024]{1,0:T(8,128)(2,1)} %get-tuple-element.43.at_in, ...), custom_call_target="tpu_custom_call" | custom-call | tf_op jit(solution)/shard_map/total/pallas_call | solution.py:524
  197.4 3.8 %update.1 = (f32[4,4,1024]{2,1,0:T(4,128)}, f32[4,4,1024]{2,1,0:T(4,128)}, f32[4,4,1024]{2,1,0:T(4,128)}, f32[4,4,1024]{2,1,0:T(4,128)}, bf16[4,4,1024]{2,1,0:T(4,128)(2,1)}, /*index=5*/f32[1024,1024]{1,0:T(8,128)}) custom-call(f32[4,4,1024]{2,1,0:T(4,128)} %get-tuple-element.47.g_in, f32[4,4,1024]{2,1,0:T(4,128)} %bitcast.13, f32[4,4,1024]{2,1,0:T(4,128)} %bitcast.12, ...), custom_call_target="tpu_custom_call" | custom-call | tf_op jit(solution)/shard_map/update/pallas_call | solution.py:552
